TPU v7x, 256 devices: a whole 4x4x8 slice. The times are simulated.
256 devices in a mesh: seq: 16 (over z, core), head: 4 (over x), batch: 4 (over y).
Axes of the slice: x: 4, y: 4, z: 8, core: 2. Of those that a mesh axis runs over, the one named last changes fastest.
Arguments:
- queries: bfloat16 [4, 8192, 4096], P('batch', 'seq', 'head'), may hold values from -6 to 6
- key_rows: bfloat16 [4, 8192, 4096], P('batch', 'seq', 'head'), may hold values from -6 to 6
- value_rows: bfloat16 [4, 8192, 4096], P('batch', 'seq', 'head'), may hold values from -6 to 6
- head_gain: float32 [4096], P('head'), may hold values from 0.25 to 1.75
- in_proj: bfloat16 [4096, 1024], P('head'), may hold values from -0.09375 to 0.09375
- level_ids: int32 [4, 8192, 4], P('batch', 'seq'), may hold values from 0 to 2047
- level_table: bfloat16 [4, 2048, 1024], P(None, 'head'), may hold values from -6 to 6
- fine_gain: float32 [1024], replicated, may hold values from 0.25 to 1.75
- query_gain: float32 [64], replicated, may hold values from 0.5 to 3
- key_gain: float32 [64], replicated, may hold values from 0.5 to 3
- fine_qkv: bfloat16 [1024, 3072], P('seq'), may hold values from -0.1875 to 0.1875
- fine_out: bfloat16 [1024, 1024], P('seq'), may hold values from -0.1875 to 0.1875
Outputs:
- fine_hidden: bfloat16 [4, 8192, 4, 1024], P('batch', ('seq', 'head'))
All inputs are finite; a program needn't handle non-finite values.
Results may differ from a plain program's by a relative error of at most 0.013.
Values may be sent and summed in bfloat16 or wider, within the bound.
A program may use at most 128 MiB of HBM per device.

v0:
```python
import math

import jax
import jax.numpy as jnp
from jax import lax
from jax.sharding import PartitionSpec as P

HD = 128
FHEADS = 16


def prefix(value, axis, join, neutral):
    count, mine = (lax.axis_size(axis), lax.axis_index(axis))
    pieces = lax.all_gather(value, axis)
    running = jnp.full_like(value, 0) + jnp.asarray(neutral, value.dtype)

    def turn(position, running):
        longer = join(running, pieces[position])
        return jnp.where(position < mine, longer, running)

    return lax.fori_loop(0, count - 1, turn, running)


def add_states(earlier, later):
    return earlier + later


def head_norm(values, gain):
    return values * lax.rsqrt(jnp.mean(values * values, axis=-1, keepdims=True) + 1e-06) * gain


def local(
    queries,
    key_rows,
    value_rows,
    head_gain,
    in_proj,
    level_ids,
    level_table,
    fine_gain,
    query_gain,
    key_gain,
    fine_qkv,
    fine_out,
):
    tok_dev = queries.shape[1]
    width_dev = queries.shape[2]
    heads_dev = width_dev // HD
    query_blk = queries[0].reshape(tok_dev, heads_dev, HD)
    key_blk = key_rows[0].reshape(tok_dev, heads_dev, HD)
    value_blk = value_rows[0].reshape(tok_dev, heads_dev, HD)
    local_state = jnp.einsum("thd,the->hde", key_blk, value_blk, preferred_element_type=jnp.float32)
    carried = prefix(local_state, "seq", add_states, jnp.zeros_like(local_state))
    causal = jnp.arange(tok_dev)[:, None] >= jnp.arange(tok_dev)[None, :]
    scores = jnp.einsum("thd,shd->hts", query_blk, key_blk, preferred_element_type=jnp.float32)
    scores = jnp.where(causal[None], scores, jnp.zeros_like(scores)).astype(jnp.bfloat16)
    local_part = jnp.einsum("hts,she->the", scores, value_blk, preferred_element_type=jnp.float32)
    carried_part = jnp.einsum(
        "thd,hde->the", query_blk.astype(jnp.float32), carried, precision=lax.Precision.HIGHEST
    )
    mixed = local_part + carried_part
    scale = lax.rsqrt(jnp.mean(mixed * mixed, axis=-1, keepdims=True) + 1e-06)
    normed = ((mixed * scale).reshape(tok_dev, width_dev) * head_gain).astype(jnp.bfloat16)
    projected = jnp.dot(normed, in_proj, preferred_element_type=jnp.float32).astype(jnp.bfloat16)
    levels = level_table.shape[0]
    vocab_dev = level_table.shape[1]
    local_ids = level_ids[0] - lax.axis_index("head") * vocab_dev
    inside = (local_ids >= 0) & (local_ids < vocab_dev)
    safe_ids = jnp.clip(local_ids, 0, vocab_dev - 1)
    looked = jnp.stack(
        [
            jnp.take(level_table[which_level], safe_ids[:, which_level], axis=0)
            for which_level in range(levels)
        ],
        axis=1,
    )
    looked = jnp.where(inside[:, :, None], looked, jnp.zeros_like(looked))
    frames_dev = tok_dev // lax.axis_size("head")
    share_proj, share_embed = (
        lax.psum_scatter(projected, "head", scatter_dimension=0, tiled=True).astype(jnp.float32),
        lax.psum_scatter(looked, "head", scatter_dimension=0, tiled=True).astype(jnp.float32),
    )
    fine_in = share_proj[:, None, :] + share_embed
    fine_width = fine_in.shape[-1]
    fine_rows = frames_dev * levels
    flat = fine_in.reshape(fine_rows, fine_width)
    fine_scale = lax.rsqrt(jnp.mean(flat * flat, axis=-1, keepdims=True) + 1e-05)
    fine_normed = (flat * fine_scale * fine_gain).astype(jnp.bfloat16)

    def fold_rows(operand, piece):
        return jnp.dot(operand, piece, preferred_element_type=jnp.float32)

    projections = fold_rows(fine_normed, lax.all_gather(fine_qkv, "seq", axis=0, tiled=True))
    fine_dim = fine_width // FHEADS
    shaped = projections.reshape(frames_dev, levels, 3, FHEADS, fine_dim)
    query_part = head_norm(shaped[:, :, 0], query_gain)
    key_part = head_norm(shaped[:, :, 1], key_gain)
    value_part = shaped[:, :, 2]
    logits = jnp.einsum(
        "flhd,fmhd->fhlm", query_part, key_part, precision=lax.Precision.HIGHEST
    ) / math.sqrt(fine_dim)
    allowed = jnp.arange(levels)[:, None] >= jnp.arange(levels)[None, :]
    level_weights = jnp.where(allowed, jnp.exp(logits), jnp.zeros_like(logits))
    level_weights = level_weights / jnp.sum(level_weights, axis=-1, keepdims=True)
    context = jnp.einsum(
        "fhlm,fmhd->flhd", level_weights, value_part, precision=lax.Precision.HIGHEST
    )
    context = context.reshape(fine_rows, fine_width).astype(jnp.bfloat16)
    attended = fold_rows(context, lax.all_gather(fine_out, "seq", axis=0, tiled=True))
    return (flat + attended).astype(jnp.bfloat16).reshape(1, frames_dev, levels, fine_width)


def solution(mesh):
    placed = (
        P("batch", "seq", "head"),
        P("batch", "seq", "head"),
        P("batch", "seq", "head"),
        P("head"),
        P("head", None),
        P("batch", "seq", None),
        P(None, "head", None),
        P(),
        P(),
        P(),
        P("seq", None),
        P("seq", None),
    )
    return jax.shard_map(
        local,
        mesh=mesh,
        in_specs=placed,
        out_specs=P("batch", ("seq", "head"), None, None),
        check_vma=False,
    )
```

profile of v0, /device:TPU:1, one launch (start us, length us, event | category | flops | bytes accessed | tf_op | source)
XLA Modules:
  0.0 286.8 jit_solution(5296118067406804571)
XLA Ops:
  15.7 3.9 %slice_bitcast_fusion.6 = (bf16[512,1024]{1,0:T(8,128)(2,1)S(1)}, bf16[512,1024]{1,0:T(8,128)(2,1)}, bf16[512,1024]{1,0:T(8,128)(2,1)}, bf16[512,1024]{1,0:T(8,128)(2,1)}) fusion(bf16[4,512,1024]{2,1,0:T(8,128)(2,1)} %param.22), kind=kLoop, calls=%fused_computation.47 | loop fusion | bytes 8388608 | tf_op jit(solution)/shard_map/squeeze | solution.py:72
  19.6 4.8 %gather_fusion.3 = bf16[512,1024]{1,0:T(8,128)(2,1)} fusion(bf16[512,1024]{1,0:T(8,128)(2,1)} %get-tuple-element.115, s32[1024]{0:T(1024)S(1)} %pad_clamp_fusion), kind=kCustom, calls=%fused_computation.3.clone | custom fusion | bytes 2099200 | tf_op jit(solution)/shard_map/jit(_take)/gather | solution.py:72
  24.5 4.9 %gather_fusion.2 = bf16[512,1024]{1,0:T(8,128)(2,1)} fusion(bf16[512,1024]{1,0:T(8,128)(2,1)} %get-tuple-element.116, s32[1024]{0:T(1024)S(1)} %pad_clamp_fusion.1), kind=kCustom, calls=%fused_computation.2.clone | custom fusion | bytes 2099200 | tf_op jit(solution)/shard_map/jit(_take)/gather | solution.py:72
  29.3 4.8 %gather_fusion.1 = bf16[512,1024]{1,0:T(8,128)(2,1)} fusion(bf16[512,1024]{1,0:T(8,128)(2,1)} %get-tuple-element.114, s32[1024]{0:T(1024)S(1)} %pad_clamp_fusion.2), kind=kCustom, calls=%fused_computation.1.clone | custom fusion | bytes 2099200 | tf_op jit(solution)/shard_map/jit(_take)/gather | solution.py:72
  34.2 2.8 gather_fusion
  37.1 5.8 %fusion = f32[8,512,128]{1,2,0:T(8,128)} fusion(pred[512,512]{1,0:T(8,128)(4,1)S(1)} %iota_compare_fusion, bf16[512,8,128]{0,2,1:T(8,128)(2,1)} %bitcast.87, bf16[512,8,128]{2,1,0:T(8,128)(2,1)} %bitcast.89, bf16[512,8,128]{2,1,0:T(8,128)(2,1)} %bitcast.90), kind=kOutput, calls=%fused_computation.6 | convolution fusion | flops 1077936128 | bytes 5505024 | tf_op jit(solution)/shard_map/hts,she->the/dot_general | solution.py:57
  42.9 29.6 %all-gather.9.cloned.1.call-done = f32[128,128,128]{2,1,0:T(8,128)} async-done(((f32[8,128,128]{2,1,0:T(8,128)}), f32[128,128,128]{2,1,0:T(8,128)}) %all-gather.9.cloned.1.call-update) | async-done | bytes 8388624 | tf_op jit(solution)/shard_map/all_gather | solution.py:14
  72.6 18.8 %while.14 = (s32[]{:T(128)}, f32[8,128,128]{2,1,0:T(8,128)S(1)}, s32[]{:T(128)}, f32[16,8,128,128]{3,2,1,0:T(8,128)}, s32[]{:T(128)}, /*index=5*/s32[]{:T(128)}) while((s32[]{:T(128)}, f32[8,128,128]{2,1,0:T(8,128)S(1)}, s32[]{:T(128)}, f32[16,8,128,128]{3,2,1,0:T(8,128)}, s32[]{:T(128)}, /*index=5*/s32[]{:T(128)}) %tuple.60), condition=%wide.region_1.2_spmd.clone, body=%wide.region_0.1_spmd.clone.sunk | while | flops 393220 | bytes 1572965 | solution.py:21
  91.3 3.2 %multiply_reduce_fusion.3 = (f32[512,8]{0,1:T(8,128)S(1)}, f32[512,8,128]{0,2,1:T(8,128)S(1)}) fusion(f32[8,128,128]{2,1,0:T(8,128)S(1)} %get-tuple-element.85, bf16[512,8,128]{2,1,0:T(8,128)(2,1)} %bitcast.91, f32[8,512,128]{1,2,0:T(8,128)} %fusion), kind=kOutput, calls=%fused_computation.33 | convolution fusion | flops 806875136 | bytes 5783552 | tf_op jit(solution)/shard_map/thd,hde->the/dot_general | solution.py:58
  103.2 15.8 %all-gather.5.cloned.1.call-done = bf16[1024,3072]{1,0:T(8,128)(2,1)} async-done(((bf16[64,3072]{1,0:T(8,128)(2,1)}), bf16[1024,3072]{1,0:T(8,128)(2,1)}) %all-gather.5.cloned.1.call-update) | async-done | bytes 6291472 | tf_op jit(solution)/shard_map/all_gather | solution.py:93
  119.0 8.7 %copy.44 = bf16[3072,1024]{1,0:T(8,128)(2,1)} copy(bf16[3072,1024]{0,1:T(8,128)(2,1)} %bitcast.84) | data formatting | bytes 12582912 | tf_op jit(solution)/shard_map/dot_general | solution.py:91
  127.7 16.9 %reduce-scatter.3.cloned.1.call-done = bf16[128,1024]{1,0:T(8,128)(2,1)} async-done(((bf16[512,1024]{1,0:T(8,128)(2,1)}), bf16[128,1024]{1,0:T(8,128)(2,1)}) %reduce-scatter.3.cloned.1.call-update) | async-done | bytes 262160 | tf_op jit(solution)/shard_map/reduce_scatter | solution.py:80
  145.6 52.0 %reduce-scatter.5.cloned.1.call-done = bf16[128,4,1024]{2,0,1:T(8,128)(2,1)} async-done(((bf16[512,4,1024]{2,0,1:T(8,128)(2,1)}), bf16[128,4,1024]{2,0,1:T(8,128)(2,1)}) %reduce-scatter.5.cloned.1.call-update) | async-done | bytes 1048592 | tf_op jit(solution)/shard_map/reduce_scatter | solution.py:81
  199.3 7.5 %fusion.16 = f32[128,4,3,16,64]{0,4,3,2,1:T(8,128)} fusion(bf16[3,16,64,1024,1]{3,2,1,0,4:T(8,128)(2,1)} %bitcast.85, f32[1024]{0:T(1024)S(1)} %copy-done.14, f32[128,4]{0,1:T(4,128)S(1)} %add_rsqrt_fusion.3, bf16[128,4,1024]{2,0,1:T(8,128)(2,1)S(1)} %copy-done.9, f32[128,1024]{1,0:T(8,128)S(1)} %convert_element_type.35), kind=kOutput, calls=%fused_computation.37 | convolution fusion | flops 3223846912 | bytes 14161920 | tf_op jit(solution)/shard_map/dot_general | solution.py:91
  206.7 2.6 copy.43
  209.4 2.9 %reshape.101 = f32[512,1024]{1,0:T(8,128)} reshape(f32[128,4,1024]{2,1,0:T(4,128)} %copy.43) | data formatting | bytes 4194304 | tf_op jit(solution)/shard_map/reshape | solution.py:86
  214.2 3.4 %copy.47 = f32[128,4,16,64]{3,1,2,0:T(4,128)} copy(f32[128,4,16,64]{0,3,2,1:T(8,128)S(1)} %slice_bitcast_fusion.2) | data formatting | bytes 4194304 | tf_op jit(solution)/shard_map/squeeze | solution.py:98
  217.6 3.0 %multiply_reduce_fusion = (f32[128,4,16]{0,2,1:T(8,128)S(1)}, f32[128,4,16]{0,2,1:T(8,128)S(1)}) fusion(f32[128,4,3,16,64]{0,4,3,2,1:T(8,128)} %fusion.16), kind=kLoop, calls=%fused_computation.27 | loop fusion | flops 2080768 | bytes 4259840 | tf_op jit(solution)/shard_map/reduce_sum | solution.py:29
  220.7 4.6 %multiply_multiply_fusion = (f32[128,4,16,64]{0,3,2,1:T(8,128)S(1)}, f32[128,4,16,64]{0,3,2,1:T(8,128)}) fusion(f32[128,4,3,16,64]{0,4,3,2,1:T(8,128)} %fusion.16, f32[64]{0:T(128)S(1)} %copy-done.12, f32[128,4,16]{0,2,1:T(8,128)S(1)} %add_rsqrt_fusion, f32[64]{0:T(128)S(1)} %copy-done.13, f32[128,4,16]{0,2,1:T(8,128)S(1)} %add_rsqrt_fusion.1), kind=kLoop, calls=%fused_computation.26 | loop fusion | flops 2097152 | bytes 8454656 | tf_op jit(solution)/shard_map/mul | solution.py:29
  225.2 5.0 %copy.45 = f32[128,4,16,64]{3,1,2,0:T(4,128)} copy(f32[128,4,16,64]{0,3,2,1:T(8,128)} %get-tuple-element.112) | data formatting | bytes 4194304 | tf_op jit(solution)/shard_map/mul | solution.py:29
  230.2 3.4 %copy.46 = f32[128,4,16,64]{3,1,2,0:T(4,128)} copy(f32[128,4,16,64]{0,3,2,1:T(8,128)S(1)} %get-tuple-element.111) | data formatting | bytes 4194304 | tf_op jit(solution)/shard_map/mul | solution.py:29
  233.6 19.0 %fusion.7 = (f32[128,16,4]{2,1,0:T(8,128)S(1)}, f32[128,16,4,4]{2,3,1,0:T(4,128)S(1)}) fusion(pred[4,4]{0,1:T(4,128)(4,1)S(1)} %iota_compare_fusion.1, f32[128,4,16,64]{3,1,2,0:T(4,128)} %copy.45, f32[128,4,16,64]{3,1,2,0:T(4,128)} %copy.46), kind=kOutput, calls=%fused_computation.14 | convolution fusion | flops 25255936 | bytes 4358160 | tf_op jit(solution)/shard_map/flhd,fmhd->fhlm/dot_general | solution.py:99
  252.7 18.6 %convert_bitcast_fusion = bf16[128,4,16,64]{3,1,2,0:T(4,128)(2,1)S(1)} fusion(f32[128,4,16,64]{3,1,2,0:T(4,128)S(1)} %copy-done.6, f32[128,16,4,4]{2,3,1,0:T(4,128)S(1)} %get-tuple-element.126, f32[128,16,4]{2,1,0:T(8,128)S(1)} %get-tuple-element.125, pred[4,4]{0,1:T(4,128)(4,1)S(1)} %iota_compare_fusion.1), kind=kOutput, calls=%fused_computation.22 | convolution fusion | flops 25788416 | bytes 3309584 | tf_op jit(solution)/shard_map/fhlm,fmhd->flhd/dot_general | solution.py:105
  273.4 4.6 %add_convert_fusion = bf16[512,1024]{1,0:T(8,128)(2,1)} fusion(f32[512,1024]{1,0:T(8,128)} %reshape.101, bf16[512,1024]{1,0:T(8,128)(2,1)S(1)} %convert_element_type.40, bf16[1024,1024]{1,0:T(8,128)(2,1)} %all-gather.7.cloned.1.call-done), kind=kOutput, calls=%fused_computation.21 | convolution fusion | flops 1074790400 | bytes 6291456 | tf_op jit(solution)/shard_map/dot_general | solution.py:91
  (94 shorter events, 45.1 us)
Async XLA Ops:
  6.5 88.9 %copy-start = (bf16[1024,1024]{1,0:T(8,128)(2,1)S(1)}, bf16[1024,1024]{1,0:T(8,128)(2,1)}, u32[]{:S(2)}) copy-start(bf16[1024,1024]{1,0:T(8,128)(2,1)} %param.20) | copy-start | bytes 6291460
  6.5 66.0 %all-gather.9.cloned.1.call-start = ((), (), s32[]{:S(2)}) async-start(), calls=%async_computation.6 | async-start | bytes 8912896 | tf_op jit(solution)/shard_map/all_gather | solution.py:14
  8.2 4.1 %copy-start.7 = (bf16[1,512,1024]{1,2,0:T(8,128)(2,1)}, bf16[1,512,1024]{1,2,0:T(8,128)(2,1)S(1)}, u32[]{:S(2)}) copy-start(bf16[1,512,1024]{1,2,0:T(8,128)(2,1)S(1)} %copy.53) | copy-start | bytes 3145732
  10.1 1.0 copy-start.8
  12.3 3.3 %copy-start.10 = (s32[1,512,4]{1,2,0:T(4,128)S(1)}, s32[1,512,4]{1,2,0:T(4,128)}, u32[]{:S(2)}) copy-start(s32[1,512,4]{1,2,0:T(4,128)} %param.21) | copy-start | bytes 24580
  12.4 106.7 %all-gather.5.cloned.1.call-start = ((), (), s32[]{:S(2)}) async-start(), calls=%async_computation.4 | async-start | bytes 6684672 | tf_op jit(solution)/shard_map/all_gather | solution.py:93
  13.1 131.5 %reduce-scatter.3.cloned.1.call-start = ((), (), s32[]{:S(2)}) async-start(), calls=%async_computation.2 | async-start | bytes 1310720 | tf_op jit(solution)/shard_map/reduce_scatter | solution.py:80
  37.1 35.5 %copy-start.2 = (f32[8,128,128]{2,1,0:T(8,128)S(1)}, f32[8,128,128]{2,1,0:T(8,128)}, u32[]{:S(2)}) copy-start(f32[8,128,128]{2,1,0:T(8,128)} %custom-call) | copy-start | bytes 1572868
  94.5 0.7 copy-start.11
  95.4 2.6 copy-start.3
  97.7 99.8 %reduce-scatter.5.cloned.1.call-start = ((), (), s32[]{:S(2)}) async-start(), calls=%async_computation.3 | async-start | bytes 5242880 | tf_op jit(solution)/shard_map/reduce_scatter | solution.py:81
  98.0 1.7 copy-start.4
  98.1 1.9 copy-start.5
  102.6 170.8 %all-gather.7.cloned.1.call-start = ((), (), s32[]{:S(2)}) async-start(), calls=%async_computation.5 | async-start | bytes 2228224 | tf_op jit(solution)/shard_map/all_gather | solution.py:109
  127.7 71.6 %copy-start.14 = (f32[1024]{0:T(1024)S(1)}, f32[1024]{0:T(1024)}, u32[]{:S(2)}) copy-start(f32[1024]{0:T(1024)} %param.23) | copy-start | bytes 12292
  197.6 1.7 copy-start.9
  217.6 3.1 %copy-start.12 = (f32[64]{0:T(128)S(1)}, f32[64]{0:T(128)}, u32[]{:S(2)}) copy-start(f32[64]{0:T(128)} %param.25) | copy-start | bytes 772
  217.6 3.1 %copy-start.13 = (f32[64]{0:T(128)S(1)}, f32[64]{0:T(128)}, u32[]{:S(2)}) copy-start(f32[64]{0:T(128)} %param.24) | copy-start | bytes 772
  233.6 19.1 %copy-start.6 = (f32[128,4,16,64]{3,1,2,0:T(4,128)S(1)}, f32[128,4,16,64]{3,1,2,0:T(4,128)}, u32[]{:S(2)}) copy-start(f32[128,4,16,64]{3,1,2,0:T(4,128)} %copy.47) | copy-start | bytes 6291460
  273.4 6.9 %copy-start.1 = (bf16[1024,1024]{1,0:T(8,128)(2,1)S(1)}, bf16[1024,1024]{1,0:T(8,128)(2,1)}, u32[]{:S(2)}) copy-start(bf16[1024,1024]{1,0:T(8,128)(2,1)} %param.20) | copy-start | bytes 6291460
Sparse Core Ops, SparseCore 0:
  12.5 60.0 all-gather.8
  74.4 44.5 all-gather.4
  121.6 22.9 reduce-scatter.2
  147.0 50.5 reduce-scatter.4
  199.2 39.6 all-gather.6
where the time goes:
time: 288 us; the launch traced here: 287 us
  waiting for transfers between devices  116 us (40%)
  matrix products  62.3 us (22%)
  local copies, waits for them, and re-layouts  61 us (21%)
  other arithmetic  33.7 us (12%)
  between operations  13.5 us (5%)
    reduce_scatter x1, waiting for transfers between devices, local(): lax.psum_scatter(looked, 'head', scatter_dimension=0, tiled=True)  52 us
    all_gather x1, waiting for transfers between devices, prefix(): pieces = lax.all_gather(value, axis)  29.6 us
    dot_general x1, matrix products, local(): jnp.einsum('flhd,fmhd->fhlm', query_part, key_part, precision=lax.Precisi...  19 us
    dot_general x1, matrix products, local(): jnp.einsum('fhlm,fmhd->flhd', level_weights, value_part, precision=lax.Pr...  18.6 us
    select_n x15, other arithmetic, turn(): return jnp.where(position < mine, longer, running)  18.4 us
    gather x4, local copies, waits for them, and re-layouts, local(): jnp.take(level_table[which_level], safe_ids[:, which_level], axis=0)  17.3 us
    reduce_scatter x1, waiting for transfers between devices, local(): lax.psum_scatter(projected, 'head', scatter_dimension=0, tiled=True)  16.9 us
    all_gather x1, waiting for transfers between devices, local(): lax.all_gather(fine_qkv, 'seq', axis=0, tiled=True)  15.8 us
  transfers between devices with their start and end apart: 5, of which 4 were waited for; matrix products, arithmetic and copies ran while one was open for 50% of the time, Pallas kernels for 0%

commit v1 on v0

v1 whole, which is shorter than its diff:
```python
import functools
import math

import jax
import jax.numpy as jnp
from jax import lax
from jax.experimental import pallas as pl
from jax.experimental.pallas import tpu as pltpu
from jax.sharding import PartitionSpec as P

HD = 128
FHEADS = 16
CAP = 192
MESH = pl.DeviceIdType.MESH
F32 = jnp.float32
BF16 = jnp.bfloat16


def dot(a, b):
    return jnp.dot(a, b, preferred_element_type=F32)


def dot_rows(a, b):
    return lax.dot_general(a, b, (((0,), (0,)), ((), ())), preferred_element_type=F32)


def dot_cols(a, b):
    return lax.dot_general(a, b, (((1,), (1,)), ((), ())), preferred_element_type=F32)


def coarse_kernel(
    n_seq,
    n_head,
    n_bat,
    q_hbm,
    k_hbm,
    v_hbm,
    table_hbm,
    proj_hbm,
    ids_ref,
    gain_ref,
    coarse_ref,
    emb_ref,
    flag_ref,
    q_ref,
    k_ref,
    v_ref,
    table_ref,
    proj_ref,
    idb_ref,
    mixed_ref,
    state_out,
    state_in,
    carry_out,
    carry_in,
    rows_ref,
    rows_out,
    rows_in,
    part_out,
    part_in,
    flag_out,
    flag_in,
    load_sem,
    state_ssem,
    state_rsem,
    carry_ssem,
    carry_rsem,
    rows_ssem,
    rows_rsem,
    part_ssem,
    part_rsem,
    flag_ssem,
    flag_rsem,
):
    seq, head, bat = (lax.axis_index(a) for a in ("seq", "head", "batch"))
    tok, width = q_ref.shape
    heads = width // HD
    levels, vocab, df = table_ref.shape
    fr = tok // n_head
    piece = heads * HD // n_seq
    per_head = HD // piece

    loads = [
        pltpu.make_async_copy(src, dst, load_sem.at[i])
        for i, (src, dst) in enumerate(
            [(k_hbm, k_ref), (v_hbm, v_ref), (table_hbm, table_ref), (q_hbm, q_ref), (proj_hbm, proj_ref)]
        )
    ]
    for load in loads:
        load.start()

    barrier = pltpu.get_barrier_semaphore()

    def greet(axis, me, n):
        def one(t, c):
            pl.semaphore_signal(barrier, inc=1, device_id={axis: lax.rem(me + t, n)}, device_id_type=MESH)
            return c

        lax.fori_loop(1, n, one, 0)

    greet("seq", seq, n_seq)
    greet("head", head, n_head)
    greet("batch", bat, n_bat)

    for lv in range(levels):
        idb_ref[lv] = jnp.broadcast_to(ids_ref[:, lv : lv + 1], (tok, 128))

    lane = lax.broadcasted_iota(jnp.int32, (levels * fr, 128), 1)
    below = (
        lax.broadcasted_iota(jnp.int32, (levels * fr, levels * fr), 0)
        > lax.broadcasted_iota(jnp.int32, (levels * fr, levels * fr), 1)
    ).astype(BF16)

    def ids_of(dest):
        rows = pl.ds(pl.multiple_of(dest * fr, fr), fr)
        return jnp.concatenate([idb_ref[lv, rows, :] for lv in range(levels)], axis=0)

    def owned_by(dest, owner):
        ids = ids_of(dest)
        return jnp.where((ids >= owner * vocab) & (ids < (owner + 1) * vocab), 1.0, 0.0)

    def slots(dest, owner):
        mine = owned_by(dest, owner)
        rank = dot(below, mine.astype(BF16)).astype(jnp.int32)
        rank = jnp.where(mine > 0.5, rank, -1)
        wide = [(rank == lane + at).astype(F32).astype(BF16) for at in range(0, CAP, 128)]
        return jnp.concatenate(wide, axis=1)[:, :CAP]

    def most(d, worst):
        for t in range(1, n_head):
            worst = jnp.maximum(worst, jnp.sum(owned_by(d, lax.rem(d + t, n_head)), axis=0, keepdims=True))
        return worst

    worst = lax.fori_loop(0, n_head, most, jnp.zeros((1, 128), F32))
    over = jnp.where(worst > CAP, 1.0, 0.0)

    loads[0].wait()
    loads[1].wait()
    for h in range(heads):
        cols = slice(h * HD, (h + 1) * HD)
        state = dot_rows(k_ref[:, cols], v_ref[:, cols]).astype(BF16)
        for i in range(per_head):
            state_out[h * per_head + i, :piece] = state[i * piece : (i + 1) * piece]
    for p in range(n_seq):
        state_out[p, piece:] = jnp.broadcast_to(over, (16, 128)).astype(BF16)

    pl.semaphore_wait(barrier, n_seq + n_head + n_bat - 3)

    def state_copy(dest, src):
        return pltpu.make_async_remote_copy(
            src_ref=state_out.at[dest],
            dst_ref=state_in.at[src],
            send_sem=state_ssem.at[dest],
            recv_sem=state_rsem.at[src],
            device_id={"seq": dest},
            device_id_type=MESH,
        )

    def send_state(t, c):
        state_copy(lax.rem(seq + t, n_seq), seq).start()
        return c

    lax.fori_loop(1, n_seq, send_state, 0)
    state_in[seq] = state_out[seq]

    loads[2].wait()

    def look(dest, into):
        rows = pl.ds(pl.multiple_of(dest * fr, fr), fr)
        for lv in range(levels):
            ids = idb_ref[lv, rows, :] - head * vocab
            hot = jnp.concatenate(
                [(ids == lane[:fr] + at).astype(F32).astype(BF16) for at in range(0, vocab, 128)], axis=1
            )
            into[lv * fr : (lv + 1) * fr, :] = dot(hot, table_ref[lv]).astype(BF16)

    def rows_copy(t):
        return pltpu.make_async_remote_copy(
            src_ref=rows_out.at[t - 1],
            dst_ref=rows_in.at[t - 1],
            send_sem=rows_ssem.at[t - 1],
            recv_sem=rows_rsem.at[t - 1],
            device_id={"head": lax.rem(head + t, n_head)},
            device_id_type=MESH,
        )

    def send_rows(t, c):
        dest = lax.rem(head + t, n_head)
        look(dest, rows_ref)
        rows_out[t - 1] = dot_rows(slots(dest, head), rows_ref[...]).astype(BF16)
        rows_copy(t).start()
        return c

    lax.fori_loop(1, n_head, send_rows, 0)
    look(head, emb_ref)

    loads[3].wait()
    causal = lax.broadcasted_iota(jnp.int32, (fr, fr), 0) >= lax.broadcasted_iota(jnp.int32, (fr, fr), 1)

    def local_head(h, c):
        cols = pl.ds(pl.multiple_of(h * HD, HD), HD)
        for r in range(n_head):
            rows = slice(r * fr, (r + 1) * fr)
            qb = q_ref[rows, cols]
            diag = jnp.where(causal, dot_cols(qb, k_ref[rows, cols]), 0.0).astype(BF16)
            acc = dot(diag, v_ref[rows, cols])
            if r > 0:
                past = dot_cols(qb, k_ref[: r * fr, cols]).astype(BF16)
                acc = acc + dot(past, v_ref[: r * fr, cols])
            mixed_ref[rows, cols] = acc
        return c

    lax.fori_loop(0, heads, local_head, 0)

    def recv_state(t, c):
        src = lax.rem(seq + t, n_seq)
        state_copy(seq, src).wait_recv()
        return c

    lax.fori_loop(1, n_seq, recv_state, 0)
    run = jnp.zeros((piece, 128), F32)
    seen = jnp.zeros((16, 128), F32)
    for i in range(n_seq):
        carry_out[i] = run.astype(BF16)
        run = run + state_in[i, :piece].astype(F32)
        seen = jnp.maximum(seen, state_in[i, piece:].astype(F32))
    flag_out[...] = seen[:8]

    def carry_copy(dest, src):
        return pltpu.make_async_remote_copy(
            src_ref=carry_out.at[dest],
            dst_ref=carry_in.at[src],
            send_sem=carry_ssem.at[dest],
            recv_sem=carry_rsem.at[src],
            device_id={"seq": dest},
            device_id_type=MESH,
        )

    def send_carry(t, c):
        carry_copy(lax.rem(seq + t, n_seq), seq).start()
        return c

    lax.fori_loop(1, n_seq, send_carry, 0)
    carry_in[seq] = carry_out[seq]

    def flag_copy(t):
        return pltpu.make_async_remote_copy(
            src_ref=flag_out,
            dst_ref=flag_in.at[t - 1],
            send_sem=flag_ssem.at[t - 1],
            recv_sem=flag_rsem.at[t - 1],
            device_id={"batch": lax.rem(bat + t, n_bat)},
            device_id_type=MESH,
        )

    def send_flag(t, c):
        flag_copy(t).start()
        return c

    lax.fori_loop(1, n_bat, send_flag, 0)

    loads[4].wait()

    def recv_carry(t, c):
        src = lax.rem(seq + t, n_seq)
        carry_copy(seq, src).wait_recv()
        return c

    lax.fori_loop(1, n_seq, recv_carry, 0)

    def part_copy(t):
        return pltpu.make_async_remote_copy(
            src_ref=part_out.at[t - 1],
            dst_ref=part_in.at[t - 1],
            send_sem=part_ssem.at[t - 1],
            recv_sem=part_rsem.at[t - 1],
            device_id={"head": lax.rem(head + t, n_head)},
            device_id_type=MESH,
        )

    def project(dest):
        rows = pl.ds(pl.multiple_of(dest * fr, fr), fr)
        normed = []
        for h in range(heads):
            cols = slice(h * HD, (h + 1) * HD)
            carried = jnp.concatenate([carry_in[h * per_head + i] for i in range(per_head)], axis=0)
            mixed = mixed_ref[rows, cols] + dot(q_ref[rows, cols], carried)
            scale = lax.rsqrt(jnp.mean(mixed * mixed, axis=-1, keepdims=True) + 1e-06)
            normed.append((mixed * scale * gain_ref[:, cols]).astype(BF16))
        return dot(jnp.concatenate(normed, axis=1), proj_ref[...]).astype(BF16)

    def send_part(t, c):
        part_out[t - 1] = project(lax.rem(head + t, n_head))

        @pl.when(t < n_head)
        def _():
            part_copy(t).start()

        return c

    lax.fori_loop(1, n_head + 1, send_part, 0)

    def recv_rows(t, c):
        rows_copy(t).wait_recv()
        src = lax.rem(head + n_head - t, n_head)
        put = dot(slots(head, src), rows_in[t - 1])
        emb_ref[...] = (emb_ref[...].astype(F32) + put).astype(BF16)
        return c

    lax.fori_loop(1, n_head, recv_rows, 0)

    def recv_flag(t, seen):
        flag_copy(t).wait_recv()
        return jnp.maximum(seen, flag_in[t - 1])

    flag_ref[...] = lax.fori_loop(1, n_bat, recv_flag, seen[:8])

    coarse = part_out[n_head - 1].astype(F32)
    for t in range(1, n_head):
        part_copy(t).wait_recv()
        coarse = coarse + part_in[t - 1].astype(F32)
    coarse_ref[...] = coarse

    def sent(t, c):
        state_copy(lax.rem(seq + t, n_seq), seq).wait_send()
        carry_copy(lax.rem(seq + t, n_seq), seq).wait_send()
        return c

    lax.fori_loop(1, n_seq, sent, 0)
    for t in range(1, n_head):
        rows_copy(t).wait_send()
        part_copy(t).wait_send()
    for t in range(1, n_bat):
        flag_copy(t).wait_send()


def fine_kernel(
    coarse_ref, emb_ref, qkv_hbm, out_hbm, fgain_ref, qgain_ref, kgain_ref, o_ref, w_ref, wo_ref, n_ref, qkv_s, c_ref, sem
):
    fr, df = coarse_ref.shape
    rows = emb_ref.shape[0]
    levels = rows // fr
    fd = df // FHEADS
    wide = qkv_s.shape[2]
    tiles = df // wide
    loads = [
        pltpu.make_async_copy(qkv_hbm, w_ref, sem.at[0]),
        pltpu.make_async_copy(out_hbm, wo_ref, sem.at[1]),
    ]
    for load in loads:
        load.start()

    def norm(lv, c):
        at = pl.ds(pl.multiple_of(lv * fr, fr), fr)
        x = coarse_ref[...] + emb_ref[at, :].astype(F32)
        scale = lax.rsqrt(jnp.mean(x * x, axis=-1, keepdims=True) + 1e-05)
        n_ref[at, :] = (x * scale * fgain_ref[...]).astype(BF16)
        return c

    lax.fori_loop(0, levels, norm, 0)
    same = (
        lax.broadcasted_iota(jnp.int32, (wide, wide), 0) // fd == lax.broadcasted_iota(jnp.int32, (wide, wide), 1) // fd
    ).astype(F32).astype(BF16)

    def head_norm(x, gain):
        total = dot((x * x).astype(BF16), same)
        return x * lax.rsqrt(total * (1.0 / fd) + 1e-06) * gain

    loads[0].wait()
    step = 32

    def tile(j, c):
        at = pl.multiple_of(j * wide, wide)
        for part in range(3):
            y = dot(n_ref[...], w_ref[:, pl.ds(pl.multiple_of(part * df + j * wide, wide), wide)])
            if part == 0:
                y = head_norm(y, qgain_ref[...])
            elif part == 1:
                y = head_norm(y, kgain_ref[...])
            qkv_s[part] = y

        def frames(i, c):
            def get(part, lv):
                return qkv_s[part, pl.ds(pl.multiple_of(lv * fr + i * step, step), step), :]

            keys = [get(1, m) for m in range(levels)]
            vals = [get(2, m) for m in range(levels)]
            pairs = []
            for lv in range(1, levels):
                query = get(0, lv)
                pairs += [(query * keys[m]).astype(BF16) for m in range(lv + 1)]
            power = jnp.exp(dot(jnp.concatenate(pairs, axis=0), same))
            n = 0
            for lv in range(levels):
                if lv == 0:
                    ctx = vals[0]
                else:
                    es = [power[(n + m) * step : (n + m + 1) * step] for m in range(lv + 1)]
                    n += lv + 1
                    top = es[0] * vals[0]
                    bottom = es[0]
                    for m in range(1, lv + 1):
                        top = top + es[m] * vals[m]
                        bottom = bottom + es[m]
                    ctx = top / bottom
                c_ref[pl.ds(pl.multiple_of(lv * fr + i * step, step), step), pl.ds(at, wide)] = ctx.astype(BF16)
            return c

        lax.fori_loop(0, fr // step, frames, 0)
        return c

    lax.fori_loop(0, tiles, tile, 0)
    loads[1].wait()

    for lv in range(levels):
        at = slice(lv * fr, (lv + 1) * fr)

        def cols(j, c):
            to = pl.ds(pl.multiple_of(j * wide, wide), wide)
            x = coarse_ref[:, to] + emb_ref[at, to].astype(F32)
            y = x + dot(c_ref[at, :], wo_ref[:, to])
            o_ref[:, pl.ds(pl.multiple_of(lv * df + j * wide, wide), wide)] = y.astype(BF16)
            return c

        lax.fori_loop(0, tiles, cols, 0)


def missing_rows(level_ids, level_table, emb, n_head):
    levels, vocab, df = level_table.shape
    tok = level_ids.shape[0]
    fr = tok // n_head
    ids = level_ids.T.reshape(levels, n_head, fr).transpose(1, 0, 2).reshape(n_head, levels * fr)
    mine = ids - lax.axis_index("head") * vocab
    inside = (mine >= 0) & (mine < vocab)
    rank = jnp.cumsum(inside.astype(jnp.int32), axis=1) - 1
    dest = jnp.arange(n_head)[:, None]
    late = inside & (rank >= CAP) & (dest != lax.axis_index("head"))
    level = jnp.broadcast_to(jnp.arange(levels * fr)[None, :] // fr, mine.shape)
    rows = level_table[level, jnp.clip(mine, 0, vocab - 1)]
    rows = jnp.where(late[:, :, None], rows, jnp.zeros_like(rows))
    more = lax.psum_scatter(rows.reshape(n_head * levels * fr, df), "head", scatter_dimension=0, tiled=True)
    return (emb.astype(F32) + more.astype(F32)).astype(BF16)


def local(
    n_seq,
    n_head,
    n_bat,
    queries,
    key_rows,
    value_rows,
    head_gain,
    in_proj,
    level_ids,
    level_table,
    fine_gain,
    query_gain,
    key_gain,
    fine_qkv,
    fine_out,
):
    tok, width = queries.shape[1:]
    levels, vocab, df = level_table.shape
    heads = width // HD
    fr = tok // n_head
    rows = fr * levels
    piece = heads * HD // n_seq
    any_spec = pl.BlockSpec(memory_space=pl.ANY)
    vmem_spec = pl.BlockSpec(memory_space=pltpu.VMEM)
    dma = pltpu.SemaphoreType.DMA
    coarse, emb, flag = pl.pallas_call(
        functools.partial(coarse_kernel, n_seq, n_head, n_bat),
        out_shape=(
            jax.ShapeDtypeStruct((fr, df), F32),
            jax.ShapeDtypeStruct((rows, df), BF16),
            jax.ShapeDtypeStruct((8, 128), F32),
        ),
        in_specs=[any_spec] * 5 + [vmem_spec] * 2,
        out_specs=(vmem_spec,) * 3,
        scratch_shapes=[
            pltpu.VMEM((tok, width), BF16),
            pltpu.VMEM((tok, width), BF16),
            pltpu.VMEM((tok, width), BF16),
            pltpu.VMEM((levels, vocab, df), BF16),
            pltpu.VMEM((width, df), BF16),
            pltpu.VMEM((levels, tok, 128), jnp.int32),
            pltpu.VMEM((tok, width), F32),
            pltpu.VMEM((n_seq, piece + 16, 128), BF16),
            pltpu.VMEM((n_seq, piece + 16, 128), BF16),
            pltpu.VMEM((n_seq, piece, 128), BF16),
            pltpu.VMEM((n_seq, piece, 128), BF16),
            pltpu.VMEM((rows, df), BF16),
            pltpu.VMEM((n_head - 1, CAP, df), BF16),
            pltpu.VMEM((n_head - 1, CAP, df), BF16),
            pltpu.VMEM((n_head, fr, df), BF16),
            pltpu.VMEM((n_head - 1, fr, df), BF16),
            pltpu.VMEM((8, 128), F32),
            pltpu.VMEM((n_bat - 1, 8, 128), F32),
            dma((5,)),
            dma((n_seq,)),
            dma((n_seq,)),
            dma((n_seq,)),
            dma((n_seq,)),
            dma((n_head - 1,)),
            dma((n_head - 1,)),
            dma((n_head - 1,)),
            dma((n_head - 1,)),
            dma((n_bat - 1,)),
            dma((n_bat - 1,)),
        ],
        compiler_params=pltpu.CompilerParams(
            collective_id=0, has_side_effects=True, vmem_limit_bytes=60 * 1024 * 1024
        ),
        cost_estimate=pl.CostEstimate(flops=6_000_000_000, bytes_accessed=100_000_000, transcendentals=0),
    )(
        queries[0],
        key_rows[0],
        value_rows[0],
        level_table,
        in_proj,
        level_ids[0],
        head_gain.reshape(1, width),
    )
    emb = lax.cond(
        jnp.max(flag) > 0.5,
        lambda e: missing_rows(level_ids[0], level_table, e, n_head),
        lambda e: e,
        emb,
    )
    all_qkv = lax.all_gather(fine_qkv, "seq", axis=0, tiled=True)
    all_out = lax.all_gather(fine_out, "seq", axis=0, tiled=True)
    fd = df // FHEADS
    wide = 256
    result = pl.pallas_call(
        fine_kernel,
        out_shape=jax.ShapeDtypeStruct((fr, levels * df), BF16),
        in_specs=[vmem_spec] * 2 + [any_spec] * 2 + [vmem_spec] * 3,
        out_specs=vmem_spec,
        scratch_shapes=[
            pltpu.VMEM((df, 3 * df), BF16),
            pltpu.VMEM((df, df), BF16),
            pltpu.VMEM((rows, df), BF16),
            pltpu.VMEM((3, rows, wide), F32),
            pltpu.VMEM((rows, df), BF16),
            dma((2,)),
        ],
        compiler_params=pltpu.CompilerParams(vmem_limit_bytes=60 * 1024 * 1024),
    )(
        coarse,
        emb,
        all_qkv,
        all_out,
        fine_gain.reshape(1, df),
        jnp.tile(query_gain / math.sqrt(fd), wide // fd).reshape(1, wide),
        jnp.tile(key_gain, wide // fd).reshape(1, wide),
    )
    return result.reshape(1, fr, levels, df)


def solution(mesh):
    placed = (
        P("batch", "seq", "head"),
        P("batch", "seq", "head"),
        P("batch", "seq", "head"),
        P("head"),
        P("head", None),
        P("batch", "seq", None),
        P(None, "head", None),
        P(),
        P(),
        P(),
        P("seq", None),
        P("seq", None),
    )
    return jax.shard_map(
        functools.partial(local, mesh.shape["seq"], mesh.shape["head"], mesh.shape["batch"]),
        mesh=mesh,
        in_specs=placed,
        out_specs=P("batch", ("seq", "head"), None, None),
        check_vma=False,
    )
```

time: 288 us -> 174 us (0.60)
  Pallas kernels: 0 us -> 65.9 us
  matrix products: 62.3 us -> 0 us
  local copies, waits for them, and re-layouts: 61 us -> 5.49 us
  other arithmetic: 33.7 us -> 1.29 us
  waiting for transfers between devices: 116 us -> 85.6 us
    reduce_scatter x2 -> x0, waiting for transfers between devices: 68.9 us -> none  [the longest x1 52 us: local(): lax.psum_scatter(looked, 'head', scatter_dimension=0, tiled=True)]
    pallas_call x0 -> x2, Pallas kernels: none -> 65.9 us  [the longest x1 46 us: local(): pl.pallas_call(functools.partial(coarse_kernel, n_seq, n_head, n_bat), ou...]
    dot_general x8 -> x0, matrix products: 62.3 us -> none  [the longest x1 19 us: local(): jnp.einsum('flhd,fmhd->fhlm', query_part, key_part, precision=lax.Precisi...]
    all_gather x3 -> x2, waiting for transfers between devices: 45.4 us -> 84.5 us  [the longest x1 46.3 us: local(): all_qkv = lax.all_gather(fine_qkv, 'seq', axis=0, tiled=True)]
    select_n x20 -> x0, other arithmetic: 20.8 us -> none  [the longest x15 18.4 us: turn(): return jnp.where(position < mine, longer, running)]
    gather x4 -> x0, local copies, waits for them, and re-layouts: 17.3 us -> none  [local(): jnp.take(level_table[which_level], safe_ids[:, which_level], axis=0)]
    squeeze x3 -> x0, local copies, waits for them, and re-layouts: 9.15 us -> none  [the longest x2 5.22 us: local(): value_part = shaped[:, :, 2]]
    dot_general x1 -> x0, local copies, waits for them, and re-layouts: 8.66 us -> none  [fold_rows(): return jnp.dot(operand, piece, preferred_element_type=jnp.float32)]
  transfers between devices with their start and end apart: 5 -> 2, of which waited for: 4 -> 2; matrix products, arithmetic and copies ran while one was open for 50% -> 1% of each run, Pallas kernels for 0% -> 0%
where the time goes in v1:
time: 174 us
  waiting for transfers between devices  85.6 us (49%)
  Pallas kernels  65.9 us (38%)
  between operations  15.6 us (9%)
  local copies, waits for them, and re-layouts  5.49 us (3%)
    all_gather x1, waiting for transfers between devices, local(): all_qkv = lax.all_gather(fine_qkv, 'seq', axis=0, tiled=True)  46.3 us
    pallas_call x1, Pallas kernels, local(): pl.pallas_call(functools.partial(coarse_kernel, n_seq, n_head, n_bat), ou...  46 us
    all_gather x1, waiting for transfers between devices, local(): all_out = lax.all_gather(fine_out, 'seq', axis=0, tiled=True)  38.2 us
    pallas_call x1, Pallas kernels, local(): pl.pallas_call(fine_kernel, out_shape=jax.ShapeDtypeStruct((fr, levels *...  19.9 us
  transfers between devices with their start and end apart: 2, of which 2 were waited for; matrix products, arithmetic and copies ran while one was open for 1% of the time, Pallas kernels for 0%

profile of v1, /device:TPU:1, one launch (start us, length us, event | category | flops | bytes accessed | tf_op | source)
XLA Modules:
  0.0 173.9 jit_solution(10652201538154689612)
XLA Ops:
  7.4 1.5 copy.15
  8.9 0.0 copy-start
  8.9 46.0 %shard_map.118 = (f32[128,1024]{1,0:T(8,128)}, bf16[512,1024]{1,0:T(8,128)(2,1)S(1)}, f32[8,128]{1,0:T(8,128)}) custom-call(bf16[512,1024]{1,0:T(8,128)(2,1)} %bitcast.38, bf16[512,1024]{1,0:T(8,128)(2,1)} %bitcast.39, bf16[512,1024]{1,0:T(8,128)(2,1)} %bitcast.40, bf16[4,512,1024]{2,1,0:T(8,128)(2,1)} %table_hbm.1, bf16[1024,1024]{1,0:T(8,128)(2,1)} %proj_hbm.1, ...), custom_call_target="tpu_custom_call" | custom-call | flops 6000000000 | bytes 100000000 | tf_op jit(solution)/shard_map/pallas_call | solution.py:471
  55.0 1.3 reduce_max.9
  56.9 0.0 copy-done
  56.9 0.0 copy-start.2
  56.9 0.0 copy-start.1
  56.9 0.0 all-gather.5.cloned.1.call-start
  57.0 0.5 all-gather.5.cloned.1.call-update
  57.5 0.0 all-gather.3.cloned.1.call-start
  57.6 0.5 all-gather.3.cloned.1.call-update
  58.1 0.0 copy-done.2
  58.1 0.6 reshape_tile.6.qgain_ref
  58.8 0.0 copy-done.1
  58.8 0.6 reshape_tile.7.kgain_ref
  59.4 38.2 %all-gather.5.cloned.1.call-done.out_hbm = bf16[1024,1024]{1,0:T(8,128)(2,1)} async-done(((bf16[64,1024]{1,0:T(8,128)(2,1)}), bf16[1024,1024]{1,0:T(8,128)(2,1)}) %all-gather.5.cloned.1.call-update) | async-done | bytes 2097168 | tf_op jit(solution)/shard_map/all_gather | solution.py:531
  97.6 46.3 %all-gather.3.cloned.1.call-done.qkv_hbm = bf16[1024,3072]{1,0:T(8,128)(2,1)} async-done(((bf16[64,3072]{1,0:T(8,128)(2,1)}), bf16[1024,3072]{1,0:T(8,128)(2,1)}) %all-gather.3.cloned.1.call-update) | async-done | bytes 6291472 | tf_op jit(solution)/shard_map/all_gather | solution.py:530
  143.9 19.9 %shard_map.119 = bf16[128,4096]{1,0:T(8,128)(2,1)} custom-call(f32[128,1024]{1,0:T(8,128)} %get-tuple-element.21.coarse_ref, bf16[512,1024]{1,0:T(8,128)(2,1)S(1)} %get-tuple-element.28.emb_ref, bf16[1024,3072]{1,0:T(8,128)(2,1)} %all-gather.3.cloned.1.call-done.qkv_hbm, bf16[1024,1024]{1,0:T(8,128)(2,1)} %all-gather.5.cloned.1.call-done.out_hbm, ...), custom_call_target="tpu_custom_call" | custom-call | tf_op jit(solution)/shard_map/pallas_call | solution.py:534
  163.8 2.6 %reshape.214 = bf16[1,128,4,1024]{3,2,1,0:T(4,128)(2,1)} reshape(bf16[128,4096]{1,0:T(8,128)(2,1)} %shard_map.119) | data formatting | bytes 2097152 | tf_op jit(solution)/shard_map/reshape | solution.py:557
  (4 shorter events, 0.0 us)
Async XLA Ops:
  8.9 48.0 %copy-start = (s32[1,512,4]{1,2,0:T(4,128)S(1)}, s32[1,512,4]{1,2,0:T(4,128)}, u32[]{:S(2)}) copy-start(s32[1,512,4]{1,2,0:T(4,128)} %param.19) | copy-start | bytes 24580
  56.9 1.2 copy-start.2
  56.9 1.9 %copy-start.1 = (f32[64]{0:T(128)S(1)}, f32[64]{0:T(128)}, u32[]{:S(2)}) copy-start(f32[64]{0:T(128)} %param.23) | copy-start | bytes 772
  56.9 40.7 %all-gather.5.cloned.1.call-start = ((), (), s32[]{:S(2)}) async-start(), calls=%async_computation.3 | async-start | bytes 2228224 | tf_op jit(solution)/shard_map/all_gather | solution.py:531
  57.5 86.4 %all-gather.3.cloned.1.call-start = ((), (), s32[]{:S(2)}) async-start(), calls=%async_computation.2 | async-start | bytes 6684672 | tf_op jit(solution)/shard_map/all_gather | solution.py:530
Sparse Core Ops, SparseCore 1:
  59.2 38.3 all-gather.4
  99.3 44.5 all-gather.2

commit v2 on v1

--- a/solution.py
+++ b/solution.py
@@ -11,6 +11,8 @@
 HD = 128
 FHEADS = 16
 CAP = 192
+WIDE = 256
+STEP = 32
 MESH = pl.DeviceIdType.MESH
 F32 = jnp.float32
 BF16 = jnp.bfloat16
@@ -28,7 +30,8 @@
     return lax.dot_general(a, b, (((1,), (1,)), ((), ())), preferred_element_type=F32)
 
 
-def coarse_kernel(
+def layer_kernel(
+    cap,
     n_seq,
     n_head,
     n_bat,
@@ -37,11 +40,17 @@
     v_hbm,
     table_hbm,
     proj_hbm,
+    qkv_hbm,
+    out_hbm,
     ids_ref,
     gain_ref,
+    fgain_ref,
+    qgain_ref,
+    kgain_ref,
+    o_ref,
+    flag_ref,
     coarse_ref,
     emb_ref,
-    flag_ref,
     q_ref,
     k_ref,
     v_ref,
@@ -71,19 +80,28 @@
     part_rsem,
     flag_ssem,
     flag_rsem,
+    w_ref,
+    wo_ref,
+    n_ref,
+    c_ref,
+    qkv_s,
+    w_ssem,
+    w_rsem,
 ):
     seq, head, bat = (lax.axis_index(a) for a in ("seq", "head", "batch"))
     tok, width = q_ref.shape
     heads = width // HD
     levels, vocab, df = table_ref.shape
     fr = tok // n_head
+    n_z = n_seq // 2
+    z, core = seq // 2, lax.rem(seq, 2)
     piece = heads * HD // n_seq
     per_head = HD // piece
 
     loads = [
         pltpu.make_async_copy(src, dst, load_sem.at[i])
         for i, (src, dst) in enumerate(
-            [(k_hbm, k_ref), (v_hbm, v_ref), (table_hbm, table_ref), (q_hbm, q_ref), (proj_hbm, proj_ref)]
+            [(k_hbm, k_ref), (v_hbm, v_ref), (table_hbm, table_ref), (q_hbm, q_ref), (proj_hbm, proj_ref), (qkv_hbm, w_ref.at[z, core]), (out_hbm, wo_ref.at[z, core])]
         )
     ]
     for load in loads:
@@ -123,8 +141,8 @@
         mine = owned_by(dest, owner)
         rank = dot(below, mine.astype(BF16)).astype(jnp.int32)
         rank = jnp.where(mine > 0.5, rank, -1)
-        wide = [(rank == lane + at).astype(F32).astype(BF16) for at in range(0, CAP, 128)]
-        return jnp.concatenate(wide, axis=1)[:, :CAP]
+        wide = [(rank == lane + at).astype(F32).astype(BF16) for at in range(0, cap, 128)]
+        return jnp.concatenate(wide, axis=1)[:, :cap]
 
     def most(d, worst):
         for t in range(1, n_head):
@@ -132,7 +150,120 @@
         return worst
 
     worst = lax.fori_loop(0, n_head, most, jnp.zeros((1, 128), F32))
-    over = jnp.where(worst > CAP, 1.0, 0.0)
+    over = jnp.where(worst > cap, 1.0, 0.0)
+
+    mats = ((qkv_hbm, w_ref), (out_hbm, wo_ref))
+
+    def turn(n):
+        return lax.rem(n_z + (2 * lax.rem(n, 2) - 1) * ((n + 1) // 2), n_z)
+
+    def quarter(m, b):
+        wide = mats[m][1].shape[3] // n_bat
+        return pl.ds(pl.multiple_of(lax.rem(b, n_bat) * wide, wide), wide)
+
+    def weight_copy(m, kind, n, src, dst, device):
+        return pltpu.make_async_remote_copy(
+            src_ref=src,
+            dst_ref=dst,
+            send_sem=w_ssem.at[m, kind, n],
+            recv_sem=w_rsem.at[m, kind, n],
+            device_id=device,
+            device_id_type=MESH,
+        )
+
+    def along_z(m, n):
+        cols = quarter(m, bat)
+        to = lax.rem(z + turn(n), n_z)
+        return weight_copy(
+            m, 0, n, mats[m][0].at[:, cols], mats[m][1].at[z, core, :, cols], {"seq": 2 * to + core}
+        )
+
+    def block(n):
+        return lax.rem(z + n_z - turn(n), n_z)
+
+    def arrived_z(m, n):
+        cols = quarter(m, bat)
+        here = mats[m][1].at[block(n), core, :, cols]
+        weight_copy(m, 0, n, here, here, {"seq": seq}).wait_recv()
+
+    def along_y(m, n, side):
+        here = mats[m][1].at[block(n), core, :, quarter(m, bat)]
+        return weight_copy(m, 1 + side, n, here, here, {"batch": lax.rem(bat + (1, n_bat - 1)[side], n_bat)})
+
+    def came_y(m, n, side):
+        here = mats[m][1].at[block(n), core, :, quarter(m, bat + (n_bat - 1, 1)[side])]
+        return weight_copy(m, 1 + side, n, here, here, {"batch": bat})
+
+    def pass_y(m, n, side):
+        half = mats[m][1].shape[2] // 2
+        here = mats[m][1].at[
+            block(n), core, side * half : (side + 1) * half, quarter(m, bat + (n_bat - 1, 1)[side])
+        ]
+        return weight_copy(m, 3 + side, n, here, here, {"batch": lax.rem(bat + (1, n_bat - 1)[side], n_bat)})
+
+    def passed_y(m, n, side):
+        half = mats[m][1].shape[2] // 2
+        here = mats[m][1].at[block(n), core, side * half : (side + 1) * half, quarter(m, bat + 2)]
+        return weight_copy(m, 3 + side, n, here, here, {"batch": bat})
+
+    def across(m, n):
+        here = mats[m][1].at[block(n), core]
+        return weight_copy(m, 5, n, here, here, {"seq": 2 * z + 1 - core})
+
+    def over_blocks(first, last, act):
+        def one(n, c):
+            act(n)
+            return c
+
+        lax.fori_loop(first, last, one, 0)
+
+    def send_z(m, first, last):
+        over_blocks(first, last, lambda n: along_z(m, n).start())
+
+    def send_y(m, first, last):
+        def act(n):
+            arrived_z(m, n)
+            for side in range(2):
+                along_y(m, n, side).start()
+
+        over_blocks(first, last, act)
+
+    def send_on(m, first, last):
+        def act(n):
+            for side in range(2):
+                came_y(m, n, side).wait_recv()
+                pass_y(m, n, side).start()
+
+        over_blocks(first, last, act)
+
+    def send_across(m, first, last):
+        def act(n):
+            for side in range(2):
+                passed_y(m, n, side).wait_recv()
+            across(m, n).start()
+
+        over_blocks(first, last, act)
+
+    def got_across(m):
+        def act(n):
+            here = mats[m][1].at[block(n), 1 - core]
+            weight_copy(m, 5, n, here, here, {"seq": seq}).wait_recv()
+
+        over_blocks(0, n_z, act)
+
+    def all_sent(m):
+        def act(n):
+            along_z(m, n).wait_send()
+            for side in range(2):
+                along_y(m, n, side).wait_send()
+                pass_y(m, n, side).wait_send()
+            across(m, n).wait_send()
+
+        across(m, 0).wait_send()
+        over_blocks(1, n_z, act)
+
+    pl.semaphore_wait(barrier, n_seq + n_head + n_bat - 3)
+    send_z(0, 1, 3)
 
     loads[0].wait()
     loads[1].wait()
@@ -144,8 +275,6 @@
     for p in range(n_seq):
         state_out[p, piece:] = jnp.broadcast_to(over, (16, 128)).astype(BF16)
 
-    pl.semaphore_wait(barrier, n_seq + n_head + n_bat - 3)
-
     def state_copy(dest, src):
         return pltpu.make_async_remote_copy(
             src_ref=state_out.at[dest],
@@ -162,6 +291,9 @@
 
     lax.fori_loop(1, n_seq, send_state, 0)
     state_in[seq] = state_out[seq]
+    send_z(0, 3, 5)
+    loads[5].wait()
+    across(0, 0).start()
 
     loads[2].wait()
 
@@ -192,6 +324,7 @@
         return c
 
     lax.fori_loop(1, n_head, send_rows, 0)
+    send_y(0, 1, 3)
     look(head, emb_ref)
 
     loads[3].wait()
@@ -242,6 +375,10 @@
 
     lax.fori_loop(1, n_seq, send_carry, 0)
     carry_in[seq] = carry_out[seq]
+    send_z(0, 5, n_z)
+    send_z(1, 1, n_z)
+    loads[6].wait()
+    across(1, 0).start()
 
     def flag_copy(t):
         return pltpu.make_async_remote_copy(
@@ -258,7 +395,8 @@
         return c
 
     lax.fori_loop(1, n_bat, send_flag, 0)
-
+    send_on(0, 1, 3)
+    send_y(0, 3, 5)
     loads[4].wait()
 
     def recv_carry(t, c):
@@ -300,6 +438,10 @@
 
     lax.fori_loop(1, n_head + 1, send_part, 0)
 
+    send_on(0, 3, 5)
+    send_y(0, 5, n_z)
+    send_across(0, 1, 5)
+
     def recv_rows(t, c):
         rows_copy(t).wait_recv()
         src = lax.rem(head + n_head - t, n_head)
@@ -308,6 +450,9 @@
         return c
 
     lax.fori_loop(1, n_head, recv_rows, 0)
+    send_on(0, 5, n_z)
+    send_y(1, 1, n_z)
+    send_across(0, 5, n_z)
 
     def recv_flag(t, seen):
         flag_copy(t).wait_recv()
@@ -321,34 +466,7 @@
         coarse = coarse + part_in[t - 1].astype(F32)
     coarse_ref[...] = coarse
 
-    def sent(t, c):
-        state_copy(lax.rem(seq + t, n_seq), seq).wait_send()
-        carry_copy(lax.rem(seq + t, n_seq), seq).wait_send()
-        return c
-
-    lax.fori_loop(1, n_seq, sent, 0)
-    for t in range(1, n_head):
-        rows_copy(t).wait_send()
-        part_copy(t).wait_send()
-    for t in range(1, n_bat):
-        flag_copy(t).wait_send()
-
-
-def fine_kernel(
-    coarse_ref, emb_ref, qkv_hbm, out_hbm, fgain_ref, qgain_ref, kgain_ref, o_ref, w_ref, wo_ref, n_ref, qkv_s, c_ref, sem
-):
-    fr, df = coarse_ref.shape
-    rows = emb_ref.shape[0]
-    levels = rows // fr
     fd = df // FHEADS
-    wide = qkv_s.shape[2]
-    tiles = df // wide
-    loads = [
-        pltpu.make_async_copy(qkv_hbm, w_ref, sem.at[0]),
-        pltpu.make_async_copy(out_hbm, wo_ref, sem.at[1]),
-    ]
-    for load in loads:
-        load.start()
 
     def norm(lv, c):
         at = pl.ds(pl.multiple_of(lv * fr, fr), fr)
@@ -359,20 +477,26 @@
 
     lax.fori_loop(0, levels, norm, 0)
     same = (
-        lax.broadcasted_iota(jnp.int32, (wide, wide), 0) // fd == lax.broadcasted_iota(jnp.int32, (wide, wide), 1) // fd
-    ).astype(F32).astype(BF16)
+        (
+            lax.broadcasted_iota(jnp.int32, (WIDE, WIDE), 0) // fd
+            == lax.broadcasted_iota(jnp.int32, (WIDE, WIDE), 1) // fd
+        )
+        .astype(F32)
+        .astype(BF16)
+    )
 
     def head_norm(x, gain):
         total = dot((x * x).astype(BF16), same)
         return x * lax.rsqrt(total * (1.0 / fd) + 1e-06) * gain
 
-    loads[0].wait()
-    step = 32
+    got_across(0)
+    send_on(1, 1, n_z)
 
     def tile(j, c):
-        at = pl.multiple_of(j * wide, wide)
+        at = pl.multiple_of(j * WIDE, WIDE)
         for part in range(3):
-            y = dot(n_ref[...], w_ref[:, pl.ds(pl.multiple_of(part * df + j * wide, wide), wide)])
+            cols = pl.ds(pl.multiple_of(part * df + j * WIDE, WIDE), WIDE)
+            y = dot(n_ref[...], w_ref[:, :, :, cols].reshape(df, WIDE))
             if part == 0:
                 y = head_norm(y, qgain_ref[...])
             elif part == 1:
@@ -381,7 +505,7 @@
 
         def frames(i, c):
             def get(part, lv):
-                return qkv_s[part, pl.ds(pl.multiple_of(lv * fr + i * step, step), step), :]
+                return qkv_s[part, pl.ds(pl.multiple_of(lv * fr + i * STEP, STEP), STEP), :]
 
             keys = [get(1, m) for m in range(levels)]
             vals = [get(2, m) for m in range(levels)]
@@ -395,7 +519,7 @@
                 if lv == 0:
                     ctx = vals[0]
                 else:
-                    es = [power[(n + m) * step : (n + m + 1) * step] for m in range(lv + 1)]
+                    es = [power[(n + m) * STEP : (n + m + 1) * STEP] for m in range(lv + 1)]
                     n += lv + 1
                     top = es[0] * vals[0]
                     bottom = es[0]
@@ -403,43 +527,46 @@
                         top = top + es[m] * vals[m]
                         bottom = bottom + es[m]
                     ctx = top / bottom
-                c_ref[pl.ds(pl.multiple_of(lv * fr + i * step, step), step), pl.ds(at, wide)] = ctx.astype(BF16)
+                c_ref[pl.ds(pl.multiple_of(lv * fr + i * STEP, STEP), STEP), pl.ds(at, WIDE)] = ctx.astype(BF16)
             return c
 
-        lax.fori_loop(0, fr // step, frames, 0)
-        return c
-
-    lax.fori_loop(0, tiles, tile, 0)
-    loads[1].wait()
+        lax.fori_loop(0, fr // STEP, frames, 0)
+
+        @pl.when(j == 0)
+        def _():
+            send_across(1, 1, n_z)
+
+        return c
+
+    lax.fori_loop(0, df // WIDE, tile, 0)
+    got_across(1)
 
     for lv in range(levels):
         at = slice(lv * fr, (lv + 1) * fr)
 
         def cols(j, c):
-            to = pl.ds(pl.multiple_of(j * wide, wide), wide)
+            to = pl.ds(pl.multiple_of(j * WIDE, WIDE), WIDE)
             x = coarse_ref[:, to] + emb_ref[at, to].astype(F32)
-            y = x + dot(c_ref[at, :], wo_ref[:, to])
-            o_ref[:, pl.ds(pl.multiple_of(lv * df + j * wide, wide), wide)] = y.astype(BF16)
+            y = x + dot(c_ref[at, :], wo_ref[:, :, :, to].reshape(df, WIDE))
+            o_ref[:, pl.ds(pl.multiple_of(lv * df + j * WIDE, WIDE), WIDE)] = y.astype(BF16)
             return c
 
-        lax.fori_loop(0, tiles, cols, 0)
-
-
-def missing_rows(level_ids, level_table, emb, n_head):
-    levels, vocab, df = level_table.shape
-    tok = level_ids.shape[0]
-    fr = tok // n_head
-    ids = level_ids.T.reshape(levels, n_head, fr).transpose(1, 0, 2).reshape(n_head, levels * fr)
-    mine = ids - lax.axis_index("head") * vocab
-    inside = (mine >= 0) & (mine < vocab)
-    rank = jnp.cumsum(inside.astype(jnp.int32), axis=1) - 1
-    dest = jnp.arange(n_head)[:, None]
-    late = inside & (rank >= CAP) & (dest != lax.axis_index("head"))
-    level = jnp.broadcast_to(jnp.arange(levels * fr)[None, :] // fr, mine.shape)
-    rows = level_table[level, jnp.clip(mine, 0, vocab - 1)]
-    rows = jnp.where(late[:, :, None], rows, jnp.zeros_like(rows))
-    more = lax.psum_scatter(rows.reshape(n_head * levels * fr, df), "head", scatter_dimension=0, tiled=True)
-    return (emb.astype(F32) + more.astype(F32)).astype(BF16)
+        lax.fori_loop(0, df // WIDE, cols, 0)
+
+    all_sent(0)
+    all_sent(1)
+
+    def sent(t, c):
+        state_copy(lax.rem(seq + t, n_seq), seq).wait_send()
+        carry_copy(lax.rem(seq + t, n_seq), seq).wait_send()
+        return c
+
+    lax.fori_loop(1, n_seq, sent, 0)
+    for t in range(1, n_head):
+        rows_copy(t).wait_send()
+        part_copy(t).wait_send()
+    for t in range(1, n_bat):
+        flag_copy(t).wait_send()
 
 
 def local(
@@ -468,92 +595,78 @@
     any_spec = pl.BlockSpec(memory_space=pl.ANY)
     vmem_spec = pl.BlockSpec(memory_space=pltpu.VMEM)
     dma = pltpu.SemaphoreType.DMA
-    coarse, emb, flag = pl.pallas_call(
-        functools.partial(coarse_kernel, n_seq, n_head, n_bat),
-        out_shape=(
-            jax.ShapeDtypeStruct((fr, df), F32),
-            jax.ShapeDtypeStruct((rows, df), BF16),
-            jax.ShapeDtypeStruct((8, 128), F32),
-        ),
-        in_specs=[any_spec] * 5 + [vmem_spec] * 2,
-        out_specs=(vmem_spec,) * 3,
-        scratch_shapes=[
-            pltpu.VMEM((tok, width), BF16),
-            pltpu.VMEM((tok, width), BF16),
-            pltpu.VMEM((tok, width), BF16),
-            pltpu.VMEM((levels, vocab, df), BF16),
-            pltpu.VMEM((width, df), BF16),
-            pltpu.VMEM((levels, tok, 128), jnp.int32),
-            pltpu.VMEM((tok, width), F32),
-            pltpu.VMEM((n_seq, piece + 16, 128), BF16),
-            pltpu.VMEM((n_seq, piece + 16, 128), BF16),
-            pltpu.VMEM((n_seq, piece, 128), BF16),
-            pltpu.VMEM((n_seq, piece, 128), BF16),
-            pltpu.VMEM((rows, df), BF16),
-            pltpu.VMEM((n_head - 1, CAP, df), BF16),
-            pltpu.VMEM((n_head - 1, CAP, df), BF16),
-            pltpu.VMEM((n_head, fr, df), BF16),
-            pltpu.VMEM((n_head - 1, fr, df), BF16),
-            pltpu.VMEM((8, 128), F32),
-            pltpu.VMEM((n_bat - 1, 8, 128), F32),
-            dma((5,)),
-            dma((n_seq,)),
-            dma((n_seq,)),
-            dma((n_seq,)),
-            dma((n_seq,)),
-            dma((n_head - 1,)),
-            dma((n_head - 1,)),
-            dma((n_head - 1,)),
-            dma((n_head - 1,)),
-            dma((n_bat - 1,)),
-            dma((n_bat - 1,)),
-        ],
-        compiler_params=pltpu.CompilerParams(
-            collective_id=0, has_side_effects=True, vmem_limit_bytes=60 * 1024 * 1024
-        ),
-        cost_estimate=pl.CostEstimate(flops=6_000_000_000, bytes_accessed=100_000_000, transcendentals=0),
-    )(
+    fd = df // FHEADS
+    args = (
         queries[0],
         key_rows[0],
         value_rows[0],
         level_table,
         in_proj,
+        fine_qkv,
+        fine_out,
         level_ids[0],
         head_gain.reshape(1, width),
+        fine_gain.reshape(1, df),
+        jnp.tile(query_gain / math.sqrt(fd), WIDE // fd).reshape(1, WIDE),
+        jnp.tile(key_gain, WIDE // fd).reshape(1, WIDE),
     )
-    emb = lax.cond(
-        jnp.max(flag) > 0.5,
-        lambda e: missing_rows(level_ids[0], level_table, e, n_head),
-        lambda e: e,
-        emb,
-    )
-    all_qkv = lax.all_gather(fine_qkv, "seq", axis=0, tiled=True)
-    all_out = lax.all_gather(fine_out, "seq", axis=0, tiled=True)
-    fd = df // FHEADS
-    wide = 256
-    result = pl.pallas_call(
-        fine_kernel,
-        out_shape=jax.ShapeDtypeStruct((fr, levels * df), BF16),
-        in_specs=[vmem_spec] * 2 + [any_spec] * 2 + [vmem_spec] * 3,
-        out_specs=vmem_spec,
-        scratch_shapes=[
-            pltpu.VMEM((df, 3 * df), BF16),
-            pltpu.VMEM((df, df), BF16),
-            pltpu.VMEM((rows, df), BF16),
-            pltpu.VMEM((3, rows, wide), F32),
-            pltpu.VMEM((rows, df), BF16),
-            dma((2,)),
-        ],
-        compiler_params=pltpu.CompilerParams(vmem_limit_bytes=60 * 1024 * 1024),
-    )(
-        coarse,
-        emb,
-        all_qkv,
-        all_out,
-        fine_gain.reshape(1, df),
-        jnp.tile(query_gain / math.sqrt(fd), wide // fd).reshape(1, wide),
-        jnp.tile(key_gain, wide // fd).reshape(1, wide),
-    )
+
+    def run(cap, collective_id):
+        return pl.pallas_call(
+            functools.partial(layer_kernel, cap, n_seq, n_head, n_bat),
+            out_shape=(
+                jax.ShapeDtypeStruct((fr, levels * df), BF16),
+                jax.ShapeDtypeStruct((8, 128), F32),
+            ),
+            in_specs=[any_spec] * 7 + [vmem_spec] * 5,
+            out_specs=(vmem_spec,) * 2,
+            scratch_shapes=[
+                pltpu.VMEM((fr, df), F32),
+                pltpu.VMEM((rows, df), BF16),
+                pltpu.VMEM((tok, width), BF16),
+                pltpu.VMEM((tok, width), BF16),
+                pltpu.VMEM((tok, width), BF16),
+                pltpu.VMEM((levels, vocab, df), BF16),
+                pltpu.VMEM((width, df), BF16),
+                pltpu.VMEM((levels, tok, 128), jnp.int32),
+                pltpu.VMEM((tok, width), F32),
+                pltpu.VMEM((n_seq, piece + 16, 128), BF16),
+                pltpu.VMEM((n_seq, piece + 16, 128), BF16),
+                pltpu.VMEM((n_seq, piece, 128), BF16),
+                pltpu.VMEM((n_seq, piece, 128), BF16),
+                pltpu.VMEM((rows, df), BF16),
+                pltpu.VMEM((n_head - 1, cap, df), BF16),
+                pltpu.VMEM((n_head - 1, cap, df), BF16),
+                pltpu.VMEM((n_head, fr, df), BF16),
+                pltpu.VMEM((n_head - 1, fr, df), BF16),
+                pltpu.VMEM((8, 128), F32),
+                pltpu.VMEM((n_bat - 1, 8, 128), F32),
+                dma((7,)),
+                dma((n_seq,)),
+                dma((n_seq,)),
+                dma((n_seq,)),
+                dma((n_seq,)),
+                dma((n_head - 1,)),
+                dma((n_head - 1,)),
+                dma((n_head - 1,)),
+                dma((n_head - 1,)),
+                dma((n_bat - 1,)),
+                dma((n_bat - 1,)),
+                pltpu.VMEM((n_seq // 2, 2, df // n_seq, 3 * df), BF16),
+                pltpu.VMEM((n_seq // 2, 2, df // n_seq, df), BF16),
+                pltpu.VMEM((rows, df), BF16),
+                pltpu.VMEM((rows, df), BF16),
+                pltpu.VMEM((3, rows, WIDE), F32),
+                dma((2, 6, n_seq // 2)),
+                dma((2, 6, n_seq // 2)),
+            ],
+            compiler_params=pltpu.CompilerParams(
+                collective_id=collective_id, has_side_effects=True, vmem_limit_bytes=60 * 1024 * 1024
+            ),
+        )(*args)
+
+    result, over = run(CAP, 0)
+    result = lax.cond(over[0, 0] > 0.5, lambda r: run(rows, 1)[0], lambda r: r, result)
     return result.reshape(1, fr, levels, df)
 
 

time: 174 us -> 86.7 us (0.50)
  waiting for transfers between devices: 85.6 us -> 0 us
  between operations: 15.6 us -> 0.78 us
  Pallas kernels: 65.9 us -> 79.1 us
    all_gather x2 -> x0, waiting for transfers between devices: 84.5 us -> none  [the longest x1 46.3 us: local(): all_qkv = lax.all_gather(fine_qkv, 'seq', axis=0, tiled=True)]
    pallas_call x2 -> x1, Pallas kernels: 65.9 us -> 79.1 us  [run(): pl.pallas_call(functools.partial(layer_kernel, cap, n_seq, n_head, n_bat)...]
  transfers between devices with their start and end apart: 2 -> 0, of which waited for: 2 -> 0; matrix products, arithmetic and copies ran while one was open for 1% -> 0% of each run, Pallas kernels for 0% -> 0%
where the time goes in v2:
time: 86.7 us; the launch traced here: 86.4 us
  Pallas kernels  79.1 us (91%)
  local copies, waits for them, and re-layouts  5.71 us (7%)
    pallas_call x1, Pallas kernels, run(): pl.pallas_call(functools.partial(layer_kernel, cap, n_seq, n_head, n_bat)...  79.1 us
    reshape x1, local copies, waits for them, and re-layouts, local(): return result.reshape(1, fr, levels, df)  1.85 us
    unnamed x15, local copies, waits for them, and re-layouts  1.84 us

profile of v2, /device:TPU:1, one launch (start us, length us, event | category | flops | bytes accessed | tf_op | source)
XLA Modules:
  0.0 86.4 jit_solution(14904026775442871133)
XLA Ops:
  0.0 0.7 broadcast_multiply_fusion
  0.7 0.1 reshape_tile.6.qgain_ref
  0.7 0.7 tile.5
  1.4 0.1 reshape_tile.7.kgain_ref
  1.5 0.8 copy.15
  2.3 0.0 copy-start
  2.3 0.0 copy-start.1
  2.4 0.0 copy-start.2
  2.4 0.0 copy-start.4
  2.4 0.0 copy-start.5
  2.4 0.0 copy-start.6
  2.4 79.1 %shard_map.120 = (bf16[128,4096]{1,0:T(8,128)(2,1)}, f32[8,128]{1,0:T(8,128)}) custom-call(bf16[512,1024]{1,0:T(8,128)(2,1)} %bitcast.7, bf16[512,1024]{1,0:T(8,128)(2,1)} %bitcast.9, bf16[512,1024]{1,0:T(8,128)(2,1)} %bitcast.11, bf16[4,512,1024]{2,1,0:T(8,128)(2,1)} %table_hbm.1, bf16[1024,1024]{1,0:T(8,128)(2,1)} %proj_hbm.1, bf16[64,3072]{1,0:T(8,128)(2,1)} %qkv_hbm.1, ...), custom_call_target="tpu_custom_call" | custom-call | tf_op jit(solution)/shard_map/pallas_call | solution.py:615
  81.5 1.2 %slice.3 = f32[1,1]{1,0:T(1,128)} slice(f32[8,128]{1,0:T(8,128)} %get-tuple-element.50), slice={[0:1], [0:1]} | slice | bytes 8 | tf_op jit(solution)/shard_map/slice | solution.py:669
  83.3 0.0 copy-done
  83.3 0.0 copy-done.1
  83.4 0.0 copy-done.2
  83.4 0.0 copy-done.4
  83.4 0.0 copy-done.5
  83.4 0.0 copy-done.6
  83.4 2.0 %conditional.1 = (bf16[1,128,4,1024]{3,2,1,0:T(4,128)(2,1)S(1)}) conditional(s32[]{:T(128)} %bitcast.6, bf16[128,4096]{1,0:T(8,128)(2,1)} %get-tuple-element.51, (bf16[512,1024]{1,0:T(8,128)(2,1)S(1)}, bf16[512,1024]{1,0:T(8,128)(2,1)}, bf16[512,1024]{1,0:T(8,128)(2,1)}, bf16[4,512,1024]{2,1,0:T(8,128)(2,1)}, bf16[1024,1024]{1,0:T(8,128)(2,1)S(1)}, ...), branch_computations={%region_0.0_spmd, %region_1.0_spmd} | conditional | bytes 2097160 | solution.py:669
  83.4 1.9 %reshape.15 = bf16[1,128,4,1024]{3,2,1,0:T(4,128)(2,1)S(1)} reshape(bf16[128,4096]{1,0:T(8,128)(2,1)} %param) | data formatting | bytes 2097152 | tf_op jit(solution)/shard_map/reshape | solution.py:670
  85.4 0.0 copy-start.3
  85.5 1.0 %copy-done.3 = bf16[1,128,4,1024]{3,2,1,0:T(4,128)(2,1)} copy-done((bf16[1,128,4,1024]{3,2,1,0:T(4,128)(2,1)}, bf16[1,128,4,1024]{3,2,1,0:T(4,128)(2,1)S(1)}, u32[]{:S(2)}) %copy-start.3) | copy-done | bytes 1048600
  (1 shorter events, 0.0 us)
Async XLA Ops:
  2.3 81.0 %copy-start = (bf16[1024,1024]{1,0:T(8,128)(2,1)S(1)}, bf16[1024,1024]{1,0:T(8,128)(2,1)}, u32[]{:S(2)}) copy-start(bf16[1024,1024]{1,0:T(8,128)(2,1)} %proj_hbm.1) | copy-start | bytes 6291460
  2.3 81.0 %copy-start.1 = (bf16[1,512,1024]{2,1,0:T(8,128)(2,1)S(1)}, bf16[1,512,1024]{2,1,0:T(8,128)(2,1)}, u32[]{:S(2)}) copy-start(bf16[1,512,1024]{2,1,0:T(8,128)(2,1)} %param.14) | copy-start | bytes 3145732
  2.4 81.0 %copy-start.2 = (bf16[64,3072]{1,0:T(8,128)(2,1)S(1)}, bf16[64,3072]{1,0:T(8,128)(2,1)}, u32[]{:S(2)}) copy-start(bf16[64,3072]{1,0:T(8,128)(2,1)} %qkv_hbm.1) | copy-start | bytes 1179652
  2.4 81.0 %copy-start.4 = (bf16[64,1024]{1,0:T(8,128)(2,1)S(1)}, bf16[64,1024]{1,0:T(8,128)(2,1)}, u32[]{:S(2)}) copy-start(bf16[64,1024]{1,0:T(8,128)(2,1)} %out_hbm.1) | copy-start | bytes 393220
  2.4 81.0 %copy-start.5 = (f32[1024]{0:T(1024)S(1)}, f32[1024]{0:T(1024)}, u32[]{:S(2)}) copy-start(f32[1024]{0:T(1024)} %param.17) | copy-start | bytes 12292
  2.4 81.0 %copy-start.6 = (f32[1024]{0:T(1024)S(1)}, f32[1024]{0:T(1024)}, u32[]{:S(2)}) copy-start(f32[1024]{0:T(1024)} %param.21) | copy-start | bytes 12292
  85.4 1.0 %copy-start.3 = (bf16[1,128,4,1024]{3,2,1,0:T(4,128)(2,1)}, bf16[1,128,4,1024]{3,2,1,0:T(4,128)(2,1)S(1)}, u32[]{:S(2)}) copy-start(bf16[1,128,4,1024]{3,2,1,0:T(4,128)(2,1)S(1)} %get-tuple-element.55) | copy-start | bytes 3145732
